TPU v7x, 256 devices: a whole 4x4x8 slice. The times are simulated.
256 devices in a mesh: seq: 64 (over x, z, core), tp: 4 (over y).
Axes of the slice: x: 4, y: 4, z: 8, core: 2. Of those that a mesh axis runs over, the one named last changes fastest.
Arguments:
- queries: bfloat16 [65536, 2048], P('seq', 'tp'), may hold values from -6.5 to 6.5
- db_keys: bfloat16 [1024, 128, 2048], P('seq', None, 'tp'), may hold values from -6 to 6
- db_values: bfloat16 [1024, 128, 2048], P('seq', None, 'tp'), may hold values from -12 to 12
- nb_shard: int32 [1024, 2], P('seq'), may hold values from 0 to 63, all different within a row; in each aligned block of 16 rows (0 to 15, 16 to 31, ...) at most 2 rows name the same one
- nb_row: int32 [1024, 2], P('seq'), may hold values from 0 to 15
- out_weight: bfloat16 [2048, 4096], P('seq', 'tp'), may hold values from -0.125 to 0.125
Outputs:
- mixed: bfloat16 [65536, 4096], P('seq', 'tp')
Inputs may be any that keep to these rules, and one draw needn't show every extreme that they name: `nb_shard`: among the 16 blocks of one index of seq no shard is named more than 2 times, a bound that some block reaches in some such group; the 2 shards of one block differ.
All inputs are finite; a program needn't handle non-finite values.
Results may differ from a plain program's by a relative error of at most 0.024.
Values may be sent and summed in bfloat16 or wider, within the bound.
No kernel may reach another device: no remote copies, remote signals or barrier semaphores. Data moves between devices by JAX's collectives and lax.ppermute only.
A program may use at most 192 MiB of HBM per device.

v0:
```python
import jax
import jax.numpy as jnp
from jax import lax
from jax.sharding import PartitionSpec as P

HD = 128
BLOCK = 64
NBR = 2
NLEN = 128


def from_behind(shard, axis, by):
    count = lax.axis_size(axis)
    pairs = [(i, i + by) for i in range(count) if 0 <= i + by < count]
    return lax.ppermute(shard, axis, pairs)


def per_device(queries, db_keys, db_values, nb_shard, nb_row, out_weight):
    score_scale = float(HD) ** (-0.5)
    tok_rows = queries.shape[0]
    feature_cols = queries.shape[1]
    heads_here = feature_cols // HD
    blocks = tok_rows // BLOCK
    shards = lax.axis_size("seq")
    capacity = max(2, 4 * blocks // shards)
    upcoming = from_behind(queries[:BLOCK], "seq", -1)
    extended = jnp.concatenate([queries[BLOCK - 1 :], upcoming[: BLOCK - 1]], axis=0).reshape(
        blocks, BLOCK, feature_cols
    )
    owners = nb_shard.reshape(-1)
    entries = nb_row.reshape(-1)
    requests = owners.shape[0]
    positions = jnp.arange(requests, dtype=jnp.int32)
    same_owner = (owners[:, None] == owners[None, :]) & (positions[None, :] < positions[:, None])
    slot_rank = jnp.sum(same_owner.astype(jnp.int32), axis=1)
    slot_index = owners * capacity + slot_rank
    outgoing = (
        jnp.zeros((shards * capacity, BLOCK, feature_cols), jnp.bfloat16)
        .at[slot_index]
        .set(extended[positions // NBR])
    )
    outgoing = outgoing.reshape(shards, capacity, BLOCK, feature_cols)
    wanted = (
        jnp.zeros((shards * capacity,), jnp.int32)
        .at[slot_index]
        .set(entries)
        .reshape(shards, capacity)
    )
    asked_queries = lax.all_to_all(outgoing, "seq", split_axis=0, concat_axis=0, tiled=True)
    asked_rows = lax.all_to_all(wanted, "seq", split_axis=0, concat_axis=0, tiled=True)
    sources = asked_rows.shape[0]
    slots_in = asked_rows.shape[1]
    key_rows = db_keys[asked_rows].reshape(sources, slots_in, NLEN, heads_here, HD)
    value_rows = db_values[asked_rows].reshape(sources, slots_in, NLEN, heads_here, HD)
    query_heads = asked_queries.reshape(sources, slots_in, BLOCK, heads_here, HD)
    scores = (
        jnp.einsum("scqhd,sckhd->schqk", query_heads, key_rows, preferred_element_type=jnp.float32)
        * score_scale
    )
    row_max = jnp.max(scores, axis=-1, keepdims=True)
    log_total = row_max[..., 0] + jnp.log(jnp.sum(jnp.exp(scores - row_max), axis=-1))
    weights = jnp.exp(scores - log_total[..., None]).astype(jnp.bfloat16)
    partial_value = jnp.einsum(
        "schqk,sckhd->scqhd", weights, value_rows, preferred_element_type=jnp.float32
    )
    partial_value = partial_value.astype(jnp.bfloat16).reshape(
        sources, slots_in, BLOCK, feature_cols
    )
    partials = lax.all_to_all(partial_value, "seq", split_axis=0, concat_axis=0, tiled=True)
    log_totals = lax.all_to_all(
        log_total.astype(jnp.bfloat16), "seq", split_axis=0, concat_axis=0, tiled=True
    ).astype(log_total.dtype)
    partials = partials.reshape(shards * capacity, BLOCK, feature_cols)[slot_index]
    partials = partials.reshape(blocks, NBR, BLOCK, heads_here, HD)
    log_totals = log_totals.reshape(shards * capacity, heads_here, BLOCK)[slot_index]
    log_totals = log_totals.reshape(blocks, NBR, heads_here, BLOCK)
    best_log = jnp.max(log_totals, axis=1, keepdims=True)
    merged_log = best_log + jnp.log(jnp.sum(jnp.exp(log_totals - best_log), axis=1, keepdims=True))
    share = jnp.transpose(jnp.exp(log_totals - merged_log), (0, 1, 3, 2))[..., None]
    attended = jnp.sum(share * partials.astype(jnp.float32), axis=1).astype(jnp.bfloat16)
    attended = attended.reshape(blocks * BLOCK, feature_cols)
    tail_rows = from_behind(attended[-BLOCK:], "seq", 1)
    placed = jnp.concatenate([tail_rows[1:], attended[: tok_rows - (BLOCK - 1)]], axis=0)
    rows_all = lax.all_gather(out_weight, "seq", axis=0, tiled=True)
    own_rows = lax.all_to_all(rows_all, "tp", split_axis=0, concat_axis=1, tiled=True)
    terms = jnp.dot(placed, own_rows, preferred_element_type=jnp.float32)
    mixed = lax.psum_scatter(terms.astype(jnp.bfloat16), "tp", scatter_dimension=1, tiled=True)
    return mixed


def solution(mesh):
    placed = (
        P("seq", "tp"),
        P("seq", None, "tp"),
        P("seq", None, "tp"),
        P("seq", None),
        P("seq", None),
        P("seq", "tp"),
    )
    return jax.shard_map(
        per_device, mesh=mesh, in_specs=placed, out_specs=P("seq", "tp"), check_vma=False
    )
```

profile of v0, /device:TPU:1, one launch (start us, length us, event | category | flops | bytes accessed | tf_op | source)
XLA Modules:
  0.0 665.3 jit_solution(10887075580433408227)
XLA Ops:
  10.9 13.0 %all-to-all-start.1 = ((s32[64,1,2]{2,1,0:T(1,128)}), s32[64,1,2]{2,1,0:T(1,128)S(1)}, u32[]{:S(2)}, u32[]{:S(2)}) async-start(s32[64,1,2]{2,1,0:T(1,128)} %bitcast.5), calls=%async_computation.1 | async-start | bytes 65536 | tf_op jit(solution)/shard_map/all_to_all | solution.py:50
  32.6 4.2 broadcast_in_dim.4
  36.9 6.3 scatter_fusion
  43.1 10.0 %all-to-all-start = ((bf16[64,2,64,512]{3,2,1,0:T(8,128)(2,1)}), bf16[64,2,64,512]{3,2,1,0:T(8,128)(2,1)}, u32[]{:S(2)}, u32[]{:S(2)}) async-start(bf16[64,2,64,512]{3,2,1,0:T(8,128)(2,1)} %bitcast.66), calls=%async_computation | async-start | bytes 16777216 | tf_op jit(solution)/shard_map/all_to_all | solution.py:49
  53.5 7.8 %gather_fusion.1 = bf16[128,128,512]{2,1,0:T(8,128)(2,1)} fusion(bf16[16,128,512]{2,1,0:T(8,128)(2,1)S(1)} %copy-done, s32[1024]{0:T(1024)S(1)} %pad_clamp_fusion.1), kind=kCustom, calls=%fused_computation.1 | custom fusion | bytes 33554944 | tf_op jit(solution)/shard_map/gather | solution.py:53
  61.3 23.9 %reshape.170 = bf16[64,2,128,4,128]{4,3,2,1,0:T(4,128)(2,1)} reshape(bf16[128,128,512]{2,1,0:T(8,128)(2,1)} %gather_fusion.1) | data formatting | bytes 33554432 | tf_op jit(solution)/shard_map/reshape | solution.py:53
  85.2 7.9 %gather_fusion.3 = bf16[128,128,512]{2,1,0:T(8,128)(2,1)} fusion(bf16[16,128,512]{2,1,0:T(8,128)(2,1)S(1)} %copy-done.2, s32[1024]{0:T(1024)S(1)} %pad_clamp_fusion.1), kind=kCustom, calls=%fused_computation.3 | custom fusion | bytes 33554944 | tf_op jit(solution)/shard_map/gather | solution.py:54
  93.0 23.7 %reshape.174 = bf16[64,2,128,4,128]{4,3,2,1,0:T(4,128)(2,1)} reshape(bf16[128,128,512]{2,1,0:T(8,128)(2,1)} %gather_fusion.3) | data formatting | bytes 33554432 | tf_op jit(solution)/shard_map/reshape | solution.py:54
  116.7 122.2 %all-to-all-done = bf16[64,2,64,512]{3,2,1,0:T(8,128)(2,1)} async-done(((bf16[64,2,64,512]{3,2,1,0:T(8,128)(2,1)}), bf16[64,2,64,512]{3,2,1,0:T(8,128)(2,1)}, u32[]{:S(2)}, u32[]{:S(2)}) %all-to-all-start) | async-done | bytes 8388640 | tf_op jit(solution)/shard_map/all_to_all | solution.py:49
  238.9 19.9 %multiply_reduce_fusion = (f32[64,2,4,64]{3,2,1,0:T(4,128)S(1)}, f32[64,2,4,64,128]{4,3,2,1,0:T(8,128)}) fusion(bf16[64,2,128,4,128]{4,3,2,1,0:T(4,128)(2,1)} %reshape.170, bf16[64,2,64,512]{3,2,1,0:T(8,128)(2,1)} %all-to-all-done), kind=kOutput, calls=%fused_computation.13 | convolution fusion | flops 1082097664 | bytes 42074112 | tf_op jit(solution)/shard_map/scqhd,sckhd->schqk/dot_general | solution.py:57
  258.8 12.6 %exponential_reduce_fusion = f32[64,2,4,64]{3,2,1,0:T(4,128)S(1)} fusion(f32[64,2,4,64,128]{4,3,2,1,0:T(8,128)} %get-tuple-element.8, f32[64,2,4,64]{3,2,1,0:T(4,128)S(1)} %get-tuple-element.7), kind=kLoop, calls=%fused_computation.12 | loop fusion | flops 12550144 | bytes 17039360 | tf_op jit(solution)/shard_map/reduce_sum | solution.py:61
  272.4 5.9 all-to-all-start.2
  278.3 15.7 %convert_bitcast_fusion = bf16[64,2,4,8,8,128]{5,4,3,2,1,0:T(8,128)(2,1)} fusion(bf16[64,2,128,4,128]{4,3,2,1,0:T(4,128)(2,1)} %reshape.174, f32[64,2,4,64,128]{4,3,2,1,0:T(8,128)} %get-tuple-element.8, f32[64,2,4,64]{3,2,1,0:T(4,128)S(1)} %get-tuple-element.6), kind=kOutput, calls=%fused_computation.17 | convolution fusion | flops 1090519040 | bytes 42074112 | tf_op jit(solution)/shard_map/schqk,sckhd->scqhd/dot_general | solution.py:63
  294.0 8.4 %copy.81 = bf16[64,2,4,8,8,128]{5,4,2,3,1,0:T(8,128)(2,1)} copy(bf16[64,2,4,8,8,128]{5,4,3,2,1,0:T(8,128)(2,1)} %convert_bitcast_fusion) | data formatting | bytes 16777216 | tf_op jit(solution)/shard_map/reshape | solution.py:66
  302.4 10.5 %all-to-all-start.3 = ((bf16[64,2,64,512]{3,2,1,0:T(8,128)(2,1)}), bf16[64,2,64,512]{3,2,1,0:T(8,128)(2,1)}, u32[]{:S(2)}, u32[]{:S(2)}) async-start(bf16[64,2,64,512]{3,2,1,0:T(8,128)(2,1)} %bitcast.67), calls=%async_computation.3 | async-start | bytes 16777216 | tf_op jit(solution)/shard_map/all_to_all | solution.py:69
  313.6 106.5 %all-gather.2.cloned.1.call-done = bf16[2048,1024]{1,0:T(8,128)(2,1)} async-done(((bf16[32,1024]{1,0:T(8,128)(2,1)}), bf16[2048,1024]{1,0:T(8,128)(2,1)}) %all-gather.2.cloned.1.call-update) | async-done | bytes 4194320 | tf_op jit(solution)/shard_map/all_gather | solution.py:84
  420.2 90.8 %all-to-all-done.3 = bf16[64,2,64,512]{3,2,1,0:T(8,128)(2,1)} async-done(((bf16[64,2,64,512]{3,2,1,0:T(8,128)(2,1)}), bf16[64,2,64,512]{3,2,1,0:T(8,128)(2,1)}, u32[]{:S(2)}, u32[]{:S(2)}) %all-to-all-start.3) | async-done | bytes 8388640 | tf_op jit(solution)/shard_map/all_to_all | solution.py:69
  511.0 4.9 all-to-all-start.4
  517.3 4.1 gather_fusion.4
  524.4 5.0 multiply_reduce_fusion.1
  531.4 33.8 %all-to-all-done.4 = bf16[4,512,1024]{2,1,0:T(8,128)(2,1)} async-done(((bf16[4,512,1024]{2,1,0:T(8,128)(2,1)}), bf16[4,512,1024]{2,1,0:T(8,128)(2,1)}, u32[]{:S(2)}, u32[]{:S(2)}) %all-to-all-start.4) | async-done | bytes 4194336 | tf_op jit(solution)/shard_map/all_to_all | solution.py:85
  565.3 6.2 copy.59
  571.8 9.2 %convolution_convert_fusion = bf16[1024,4096]{1,0:T(8,128)(2,1)} fusion(bf16[512,4096]{0,1:T(8,128)(2,1)} %bitcast.71, bf16[961,512]{1,0:T(8,128)(2,1)S(1)} %slice.41, bf16[63,512]{1,0:T(8,128)(2,1)S(1)} %slice.40), kind=kOutput, calls=%fused_computation.20 | convolution fusion | flops 4301258752 | bytes 13631488 | tf_op jit(solution)/shard_map/dot_general | solution.py:86
  581.0 77.5 %reduce-scatter.2.cloned.1.call-done = bf16[1024,1024]{1,0:T(8,128)(2,1)} async-done(((bf16[1024,4096]{1,0:T(8,128)(2,1)}), bf16[1024,1024]{1,0:T(8,128)(2,1)}) %reduce-scatter.2.cloned.1.call-update) | async-done | bytes 2097168 | tf_op jit(solution)/shard_map/reduce_scatter | solution.py:87
  (55 shorter events, 21.7 us)
Async XLA Ops:
  6.5 46.9 %copy-start = (bf16[16,128,512]{2,1,0:T(8,128)(2,1)S(1)}, bf16[16,128,512]{2,1,0:T(8,128)(2,1)}, u32[]{:S(2)}) copy-start(bf16[16,128,512]{2,1,0:T(8,128)(2,1)} %param.7) | copy-start | bytes 6291460
  10.9 32.3 %all-to-all-start.1 = ((s32[64,1,2]{2,1,0:T(1,128)}), s32[64,1,2]{2,1,0:T(1,128)S(1)}, u32[]{:S(2)}, u32[]{:S(2)}) async-start(s32[64,1,2]{2,1,0:T(1,128)} %bitcast.5), calls=%async_computation.1 | async-start | bytes 65536 | tf_op jit(solution)/shard_map/all_to_all | solution.py:50
  24.7 5.9 collective-permute-start
  43.1 195.7 %all-to-all-start = ((bf16[64,2,64,512]{3,2,1,0:T(8,128)(2,1)}), bf16[64,2,64,512]{3,2,1,0:T(8,128)(2,1)}, u32[]{:S(2)}, u32[]{:S(2)}) async-start(bf16[64,2,64,512]{3,2,1,0:T(8,128)(2,1)} %bitcast.66), calls=%async_computation | async-start | bytes 16777216 | tf_op jit(solution)/shard_map/all_to_all | solution.py:49
  61.3 23.9 %copy-start.2 = (bf16[16,128,512]{2,1,0:T(8,128)(2,1)S(1)}, bf16[16,128,512]{2,1,0:T(8,128)(2,1)}, u32[]{:S(2)}) copy-start(bf16[16,128,512]{2,1,0:T(8,128)(2,1)} %param.8) | copy-start | bytes 6291460
  272.4 30.0 %all-to-all-start.2 = ((bf16[64,2,256]{2,1,0:T(2,128)(2,1)}), bf16[64,2,256]{2,1,0:T(2,128)(2,1)S(1)}, u32[]{:S(2)}, u32[]{:S(2)}) async-start(bf16[64,2,256]{2,1,0:T(2,128)(2,1)} %reshape.242), calls=%async_computation.2 | async-start | bytes 131072 | tf_op jit(solution)/shard_map/all_to_all | solution.py:70
  302.4 208.6 %all-to-all-start.3 = ((bf16[64,2,64,512]{3,2,1,0:T(8,128)(2,1)}), bf16[64,2,64,512]{3,2,1,0:T(8,128)(2,1)}, u32[]{:S(2)}, u32[]{:S(2)}) async-start(bf16[64,2,64,512]{3,2,1,0:T(8,128)(2,1)} %bitcast.67), calls=%async_computation.3 | async-start | bytes 16777216 | tf_op jit(solution)/shard_map/all_to_all | solution.py:69
  312.9 107.3 %all-gather.2.cloned.1.call-start = ((), (), s32[]{:S(2)}) async-start(), calls=%async_computation.6 | async-start | bytes 4259840 | tf_op jit(solution)/shard_map/all_gather | solution.py:84
  511.0 54.3 %all-to-all-start.4 = ((bf16[4,512,1024]{2,1,0:T(8,128)(2,1)}), bf16[4,512,1024]{2,1,0:T(8,128)(2,1)}, u32[]{:S(2)}, u32[]{:S(2)}) async-start(bf16[4,512,1024]{2,1,0:T(8,128)(2,1)} %bitcast.70), calls=%async_computation.4 | async-start | bytes 8388608 | tf_op jit(solution)/shard_map/all_to_all | solution.py:85
  515.9 142.6 %reduce-scatter.2.cloned.1.call-start = ((), (), s32[]{:S(2)}) async-start(), calls=%async_computation.7 | async-start | bytes 10485760 | tf_op jit(solution)/shard_map/reduce_scatter | solution.py:87
  529.5 42.2 %collective-permute-start.1 = (bf16[64,512]{1,0:T(8,128)(2,1)S(1)}, bf16[64,512]{1,0:T(8,128)(2,1)S(1)}, u32[]{:S(2)}, u32[]{:S(2)}) collective-permute-start(bf16[64,512]{1,0:T(8,128)(2,1)S(1)} %bitcast.78), channel_id=1, source_target_pairs={{0,4},{4,8},{8,12},{12,16},{16,20},{20,24},{24,28},{28,32},{32,36}... | collective-permute-start | bytes 196616 | tf_op jit(solution)/shard_map/ppermute | solution.py:15
  571.8 86.7 %copy-start.1 = (bf16[16,128,512]{2,1,0:T(8,128)(2,1)S(1)}, bf16[16,128,512]{2,1,0:T(8,128)(2,1)}, u32[]{:S(2)}) copy-start(bf16[16,128,512]{2,1,0:T(8,128)(2,1)} %param.7) | copy-start | bytes 6291460
Sparse Core Ops, SparseCore 0:
  316.5 103.6 all-gather.1
  581.1 77.3 reduce-scatter.1
where the time goes:
time: 667 us; the launch traced here: 665 us
  waiting for transfers between devices  434 us (65%)
  local copies, waits for them, and re-layouts  106 us (16%)
  starting transfers between devices  48.6 us (7%)
  matrix products  44.8 us (7%)
  other arithmetic  19 us (3%)
  between operations  13.7 us (2%)
    all_to_all x1, waiting for transfers between devices, per_device(): lax.all_to_all(outgoing, 'seq', split_axis=0, concat_axis=0, tiled=True)  122 us
    all_gather x1, waiting for transfers between devices, per_device(): rows_all = lax.all_gather(out_weight, 'seq', axis=0, tiled=True)  107 us
    all_to_all x1, waiting for transfers between devices, per_device(): lax.all_to_all(partial_value, 'seq', split_axis=0, concat_axis=0, tiled=T...  90.8 us
    reduce_scatter x1, waiting for transfers between devices, per_device(): lax.psum_scatter(terms.astype(jnp.bfloat16), 'tp', scatter_dimension=1, t...  77.5 us
    all_to_all x1, waiting for transfers between devices, per_device(): lax.all_to_all(rows_all, 'tp', split_axis=0, concat_axis=1, tiled=True)  33.8 us
    reshape x1, local copies, waits for them, and re-layouts, per_device(): db_keys[asked_rows].reshape(sources, slots_in, NLEN, heads_here, HD)  23.9 us
    reshape x1, local copies, waits for them, and re-layouts, per_device(): db_values[asked_rows].reshape(sources, slots_in, NLEN, heads_here, HD)  23.7 us
    dot_general x1, matrix products, per_device(): jnp.einsum('scqhd,sckhd->schqk', query_heads, key_rows, preferred_element...  19.9 us
  transfers between devices with their start and end apart: 9, of which 6 were waited for; matrix products, arithmetic and copies ran while one was open for 18% of the time, Pallas kernels for 0%

commit v1 on v0

--- a/solution.py
+++ b/solution.py
@@ -81,7 +81,16 @@
     attended = attended.reshape(blocks * BLOCK, feature_cols)
     tail_rows = from_behind(attended[-BLOCK:], "seq", 1)
     placed = jnp.concatenate([tail_rows[1:], attended[: tok_rows - (BLOCK - 1)]], axis=0)
-    rows_all = lax.all_gather(out_weight, "seq", axis=0, tiled=True)
+    try_all_tokens_by_axis = lambda local_array, mesh_ax, d_out: jnp.concatenate(
+        jax.lax.all_to_all(
+            jnp.stack([local_array for _ in range(jax.lax.axis_size(mesh_ax))], axis=0),
+            mesh_ax,
+            0,
+            0,
+        ),
+        axis=d_out,
+    )
+    rows_all = try_all_tokens_by_axis(out_weight, "seq", 0)
     own_rows = lax.all_to_all(rows_all, "tp", split_axis=0, concat_axis=1, tiled=True)
     terms = jnp.dot(placed, own_rows, preferred_element_type=jnp.float32)
     mixed = lax.psum_scatter(terms.astype(jnp.bfloat16), "tp", scatter_dimension=1, tiled=True)

time: 667 us -> 733 us (1.099)
  blocking collectives: 0 us -> 393 us
  waiting for transfers between devices: 434 us -> 114 us
  starting transfers between devices: 48.6 us -> 38.8 us
    all_to_all x0 -> x2, blocking collectives: none -> 393 us  [the longest x1 197 us: per_device(): lax.all_to_all(partial_value, 'seq', split_axis=0, concat_axis=0, tiled=T...]
    all_to_all x2 -> x1, waiting for transfers between devices: 213 us -> 0.01 us  [per_device(): jax.lax.all_to_all(jnp.stack([local_array for _ in range(jax.lax.axis_siz...]
    all_gather x1 -> x0, waiting for transfers between devices: 107 us -> none  [per_device(): rows_all = lax.all_gather(out_weight, 'seq', axis=0, tiled=True)]
    all_to_all x2 -> x1, starting transfers between devices: 20.5 us -> 6.02 us  [per_device(): jax.lax.all_to_all(jnp.stack([local_array for _ in range(jax.lax.axis_siz...]
  transfers between devices with their start and end apart: 9 -> 7, of which waited for: 6 -> 3; matrix products, arithmetic and copies ran while one was open for 18% -> 21% of each run, Pallas kernels for 0% -> 0%
where the time goes in v1:
time: 733 us; the launch traced here: 731 us
  blocking collectives  393 us (54%)
  waiting for transfers between devices  114 us (16%)
  local copies, waits for them, and re-layouts  108 us (15%)
  matrix products  44.8 us (6%)
  starting transfers between devices  38.8 us (5%)
  other arithmetic  19 us (3%)
  between operations  13.7 us (2%)
    all_to_all x1, blocking collectives, per_device(): lax.all_to_all(partial_value, 'seq', split_axis=0, concat_axis=0, tiled=T...  197 us
    all_to_all x1, blocking collectives, per_device(): lax.all_to_all(outgoing, 'seq', split_axis=0, concat_axis=0, tiled=True)  196 us
    reduce_scatter x1, waiting for transfers between devices, per_device(): lax.psum_scatter(terms.astype(jnp.bfloat16), 'tp', scatter_dimension=1, t...  78.5 us
    all_to_all x1, waiting for transfers between devices, per_device(): lax.all_to_all(rows_all, 'tp', split_axis=0, concat_axis=1, tiled=True)  32.9 us
    reshape x1, local copies, waits for them, and re-layouts, per_device(): db_keys[asked_rows].reshape(sources, slots_in, NLEN, heads_here, HD)  23.8 us
    reshape x1, local copies, waits for them, and re-layouts, per_device(): db_values[asked_rows].reshape(sources, slots_in, NLEN, heads_here, HD)  23.7 us
    dot_general x1, matrix products, per_device(): jnp.einsum('scqhd,sckhd->schqk', query_heads, key_rows, preferred_element...  19.9 us
    dot_general x1, matrix products, per_device(): jnp.einsum('schqk,sckhd->scqhd', weights, value_rows, preferred_element_t...  15.7 us
  transfers between devices with their start and end apart: 7, of which 3 were waited for; matrix products, arithmetic and copies ran while one was open for 21% of the time, Pallas kernels for 0%

profile of v1, /device:TPU:1, one launch (start us, length us, event | category | flops | bytes accessed | tf_op | source)
XLA Modules:
  0.0 730.7 jit_solution(9906214269806255350)
XLA Ops:
  10.9 13.0 %all-to-all-start.1 = ((s32[64,1,2]{2,1,0:T(1,128)}), s32[64,1,2]{2,1,0:T(1,128)S(1)}, u32[]{:S(2)}, u32[]{:S(2)}) async-start(s32[64,1,2]{2,1,0:T(1,128)} %bitcast.5), calls=%async_computation.1 | async-start | bytes 65536 | tf_op jit(solution)/shard_map/all_to_all | solution.py:50
  32.6 4.3 broadcast_in_dim.4
  36.9 6.2 scatter_fusion
  43.1 196.2 %all_to_all.51 = bf16[64,2,64,512]{3,2,1,0:T(8,128)(2,1)} all-to-all(bf16[64,2,64,512]{3,2,1,0:T(8,128)(2,1)} %bitcast.66), channel_id=1, replica_groups=mesh['seq'=64,'tp'=4] {'seq'}, dimensions={0} | all-to-all | bytes 16777216 | tf_op jit(solution)/shard_map/all_to_all | solution.py:49
  239.3 2.5 stack.2
  241.8 6.0 all-to-all-start.4
  248.1 7.8 %gather_fusion.1 = bf16[128,128,512]{2,1,0:T(8,128)(2,1)} fusion(bf16[16,128,512]{2,1,0:T(8,128)(2,1)S(1)} %copy-done, s32[1024]{0:T(1024)S(1)} %pad_clamp_fusion.1), kind=kCustom, calls=%fused_computation.1 | custom fusion | bytes 33554944 | tf_op jit(solution)/shard_map/gather | solution.py:53
  255.9 23.8 %reshape.174 = bf16[64,2,128,4,128]{4,3,2,1,0:T(4,128)(2,1)} reshape(bf16[128,128,512]{2,1,0:T(8,128)(2,1)} %gather_fusion.1) | data formatting | bytes 33554432 | tf_op jit(solution)/shard_map/reshape | solution.py:53
  279.8 7.9 %gather_fusion.3 = bf16[128,128,512]{2,1,0:T(8,128)(2,1)} fusion(bf16[16,128,512]{2,1,0:T(8,128)(2,1)S(1)} %copy-done.2, s32[1024]{0:T(1024)S(1)} %pad_clamp_fusion.1), kind=kCustom, calls=%fused_computation.3 | custom fusion | bytes 33554944 | tf_op jit(solution)/shard_map/gather | solution.py:54
  287.7 23.7 %reshape.178 = bf16[64,2,128,4,128]{4,3,2,1,0:T(4,128)(2,1)} reshape(bf16[128,128,512]{2,1,0:T(8,128)(2,1)} %gather_fusion.3) | data formatting | bytes 33554432 | tf_op jit(solution)/shard_map/reshape | solution.py:54
  311.4 19.9 %multiply_reduce_fusion = (f32[64,2,4,64]{3,2,1,0:T(4,128)S(1)}, f32[64,2,4,64,128]{4,3,2,1,0:T(8,128)}) fusion(bf16[64,2,128,4,128]{4,3,2,1,0:T(4,128)(2,1)} %reshape.174, bf16[64,2,64,512]{3,2,1,0:T(8,128)(2,1)} %all_to_all.51), kind=kOutput, calls=%fused_computation.13 | convolution fusion | flops 1082097664 | bytes 42074112 | tf_op jit(solution)/shard_map/scqhd,sckhd->schqk/dot_general | solution.py:57
  331.3 12.6 %exponential_reduce_fusion = f32[64,2,4,64]{3,2,1,0:T(4,128)S(1)} fusion(f32[64,2,4,64,128]{4,3,2,1,0:T(8,128)} %get-tuple-element.8, f32[64,2,4,64]{3,2,1,0:T(4,128)S(1)} %get-tuple-element.7), kind=kLoop, calls=%fused_computation.12 | loop fusion | flops 12550144 | bytes 17039360 | tf_op jit(solution)/shard_map/reduce_sum | solution.py:61
  344.9 10.4 %all-to-all-start.2 = ((bf16[64,2,256]{2,1,0:T(2,128)(2,1)}), bf16[64,2,256]{2,1,0:T(2,128)(2,1)S(1)}, u32[]{:S(2)}, u32[]{:S(2)}) async-start(bf16[64,2,256]{2,1,0:T(2,128)(2,1)} %reshape.246), calls=%async_computation.2 | async-start | bytes 131072 | tf_op jit(solution)/shard_map/all_to_all | solution.py:70
  355.3 15.7 %convert_bitcast_fusion = bf16[64,2,4,8,8,128]{5,4,3,2,1,0:T(8,128)(2,1)} fusion(bf16[64,2,128,4,128]{4,3,2,1,0:T(4,128)(2,1)} %reshape.178, f32[64,2,4,64,128]{4,3,2,1,0:T(8,128)} %get-tuple-element.8, f32[64,2,4,64]{3,2,1,0:T(4,128)S(1)} %get-tuple-element.6), kind=kOutput, calls=%fused_computation.17 | convolution fusion | flops 1090519040 | bytes 42074112 | tf_op jit(solution)/shard_map/schqk,sckhd->scqhd/dot_general | solution.py:63
  371.0 8.4 %copy.81 = bf16[64,2,4,8,8,128]{5,4,2,3,1,0:T(8,128)(2,1)} copy(bf16[64,2,4,8,8,128]{5,4,3,2,1,0:T(8,128)(2,1)} %convert_bitcast_fusion) | data formatting | bytes 16777216 | tf_op jit(solution)/shard_map/reshape | solution.py:66
  379.4 196.7 %all_to_all.52 = bf16[64,2,64,512]{3,2,1,0:T(8,128)(2,1)} all-to-all(bf16[64,2,64,512]{3,2,1,0:T(8,128)(2,1)} %bitcast.67), channel_id=1, replica_groups=mesh['seq'=64,'tp'=4] {'seq'}, dimensions={0} | all-to-all | bytes 16777216 | tf_op jit(solution)/shard_map/all_to_all | solution.py:69
  576.1 4.9 all-to-all-start.5
  582.4 4.1 gather_fusion.4
  586.5 3.0 reshape.183
  589.5 5.0 multiply_reduce_fusion.1
  596.6 32.9 %all-to-all-done.5 = bf16[4,512,1024]{2,1,0:T(8,128)(2,1)} async-done(((bf16[4,512,1024]{2,1,0:T(8,128)(2,1)}), bf16[4,512,1024]{2,1,0:T(8,128)(2,1)}, u32[]{:S(2)}, u32[]{:S(2)}) %all-to-all-start.5) | async-done | bytes 4194336 | tf_op jit(solution)/shard_map/all_to_all | solution.py:94
  629.6 6.2 copy.59
  636.1 9.2 %convolution_convert_fusion = bf16[1024,4096]{1,0:T(8,128)(2,1)} fusion(bf16[512,4096]{0,1:T(8,128)(2,1)} %bitcast.71, bf16[961,512]{1,0:T(8,128)(2,1)S(1)} %slice.41, bf16[63,512]{1,0:T(8,128)(2,1)S(1)} %slice.40), kind=kOutput, calls=%fused_computation.20 | convolution fusion | flops 4301258752 | bytes 13631488 | tf_op jit(solution)/shard_map/dot_general | solution.py:95
  645.3 78.5 %reduce-scatter.2.cloned.1.call-done = bf16[1024,1024]{1,0:T(8,128)(2,1)} async-done(((bf16[1024,4096]{1,0:T(8,128)(2,1)}), bf16[1024,1024]{1,0:T(8,128)(2,1)}) %reduce-scatter.2.cloned.1.call-update) | async-done | bytes 2097168 | tf_op jit(solution)/shard_map/reduce_scatter | solution.py:96
  (55 shorter events, 18.1 us)
Async XLA Ops:
  6.5 241.6 %copy-start = (bf16[16,128,512]{2,1,0:T(8,128)(2,1)S(1)}, bf16[16,128,512]{2,1,0:T(8,128)(2,1)}, u32[]{:S(2)}) copy-start(bf16[16,128,512]{2,1,0:T(8,128)(2,1)} %param.7) | copy-start | bytes 6291460
  10.9 32.3 %all-to-all-start.1 = ((s32[64,1,2]{2,1,0:T(1,128)}), s32[64,1,2]{2,1,0:T(1,128)S(1)}, u32[]{:S(2)}, u32[]{:S(2)}) async-start(s32[64,1,2]{2,1,0:T(1,128)} %bitcast.5), calls=%async_computation.1 | async-start | bytes 65536 | tf_op jit(solution)/shard_map/all_to_all | solution.py:50
  24.7 5.9 collective-permute-start
  43.1 196.2 %copy-start.3 = (bf16[32,1024]{1,0:T(8,128)(2,1)S(1)}, bf16[32,1024]{1,0:T(8,128)(2,1)}, u32[]{:S(2)}) copy-start(bf16[32,1024]{1,0:T(8,128)(2,1)} %param.11) | copy-start | bytes 196612
  241.8 103.1 %all-to-all-start.4 = ((bf16[64,32,1024]{2,1,0:T(8,128)(2,1)}), bf16[64,32,1024]{2,1,0:T(8,128)(2,1)}, u32[]{:S(2)}, u32[]{:S(2)}) async-start(bf16[64,32,1024]{2,1,0:T(8,128)(2,1)} %stack.2), calls=%async_computation.4 | async-start | bytes 8388608 | tf_op jit(solution)/shard_map/all_to_all | solution.py:85
  255.9 23.8 %copy-start.2 = (bf16[16,128,512]{2,1,0:T(8,128)(2,1)S(1)}, bf16[16,128,512]{2,1,0:T(8,128)(2,1)}, u32[]{:S(2)}) copy-start(bf16[16,128,512]{2,1,0:T(8,128)(2,1)} %param.8) | copy-start | bytes 6291460
  344.9 34.6 %all-to-all-start.2 = ((bf16[64,2,256]{2,1,0:T(2,128)(2,1)}), bf16[64,2,256]{2,1,0:T(2,128)(2,1)S(1)}, u32[]{:S(2)}, u32[]{:S(2)}) async-start(bf16[64,2,256]{2,1,0:T(2,128)(2,1)} %reshape.246), calls=%async_computation.2 | async-start | bytes 131072 | tf_op jit(solution)/shard_map/all_to_all | solution.py:70
  576.1 53.4 %all-to-all-start.5 = ((bf16[4,512,1024]{2,1,0:T(8,128)(2,1)}), bf16[4,512,1024]{2,1,0:T(8,128)(2,1)}, u32[]{:S(2)}, u32[]{:S(2)}) async-start(bf16[4,512,1024]{2,1,0:T(8,128)(2,1)} %bitcast.12), calls=%async_computation.5 | async-start | bytes 8388608 | tf_op jit(solution)/shard_map/all_to_all | solution.py:94
  581.0 142.8 %reduce-scatter.2.cloned.1.call-start = ((), (), s32[]{:S(2)}) async-start(), calls=%async_computation.7 | async-start | bytes 10485760 | tf_op jit(solution)/shard_map/reduce_scatter | solution.py:96
  594.5 41.5 %collective-permute-start.1 = (bf16[64,512]{1,0:T(8,128)(2,1)S(1)}, bf16[64,512]{1,0:T(8,128)(2,1)S(1)}, u32[]{:S(2)}, u32[]{:S(2)}) collective-permute-start(bf16[64,512]{1,0:T(8,128)(2,1)S(1)} %bitcast.78), channel_id=1, source_target_pairs={{0,4},{4,8},{8,12},{12,16},{16,20},{20,24},{24,28},{28,32},{32,36}... | collective-permute-start | bytes 196616 | tf_op jit(solution)/shard_map/ppermute | solution.py:15
  636.1 87.8 %copy-start.1 = (bf16[16,128,512]{2,1,0:T(8,128)(2,1)S(1)}, bf16[16,128,512]{2,1,0:T(8,128)(2,1)}, u32[]{:S(2)}) copy-start(bf16[16,128,512]{2,1,0:T(8,128)(2,1)} %param.7) | copy-start | bytes 6291460
Sparse Core Ops, SparseCore 0:
  645.4 78.3 reduce-scatter.1
